TPU v7x, 32 devices: a whole 2x2x4 slice. The times are simulated.
32 devices in a mesh: shard: 32 (over z, y, x, core).
Axes of the slice: x: 2, y: 2, z: 4, core: 2. Of those that a mesh axis runs over, the one named last changes fastest.
Arguments:
- hidden: bfloat16 [96, 512, 768], P('shard'), may hold values from -6 to 6
- teacher_input: bfloat16 [96, 512, 768], P('shard'), may hold values from -6 to 6
- cotangent: bfloat16 [96, 512, 768], P('shard'), may hold values from -6 to 6
- lengths: int32 [96], P('shard'), may hold values from 33 to 512, as said below
- lat_qkv: float32 [768, 2304], P('shard'), as said below
- lat_out: float32 [768, 768], P('shard'), as said below
- lat_up: float32 [768, 3072], P('shard'), as said below
- lat_down: float32 [3072, 768], P('shard'), as said below
- bias_q: float32 [768], replicated, may hold values from -0.5 to 0.5
- bias_v: float32 [768], replicated, may hold values from -0.5 to 0.5
- bias_out: float32 [768], replicated, may hold values from -0.5 to 0.5
- bias_up: float32 [3072], replicated, may hold values from -0.5 to 0.5
- bias_down: float32 [768], replicated, may hold values from -0.5 to 0.5
- gain_one: float32 [768], replicated, may hold values from 0.5 to 1.5
- shift_one: float32 [768], replicated, may hold values from -0.3 to 0.3
- gain_two: float32 [768], replicated, may hold values from 0.5 to 1.5
- shift_two: float32 [768], replicated, may hold values from -0.3 to 0.3
- clips: float32 [4], replicated, as said below
- teach_qkv: bfloat16 [768, 2304], P('shard'), may hold values from -0.21875 to 0.21875
- teach_out: bfloat16 [768, 768], P('shard'), may hold values from -1.75 to 1.75
- teach_up: bfloat16 [768, 3072], P('shard'), may hold values from -0.21875 to 0.21875
- teach_down: bfloat16 [3072, 768], P('shard'), may hold values from -0.109375 to 0.109375
Outputs:
- mixed_out: bfloat16 [96, 512, 768], P('shard')
- input_grad: bfloat16 [96, 512, 768], P('shard')
- grad_lat_qkv: float32 [768, 2304], P('shard')
- grad_lat_out: float32 [768, 768], P('shard')
- grad_lat_up: float32 [768, 3072], P('shard')
- grad_lat_down: float32 [3072, 768], P('shard')
- grad_bias_q: float32 [768], replicated
- grad_bias_v: float32 [768], replicated
- grad_bias_out: float32 [768], replicated
- grad_bias_up: float32 [3072], replicated
- grad_bias_down: float32 [768], replicated
- grad_gain_one: float32 [768], replicated
- grad_shift_one: float32 [768], replicated
- grad_gain_two: float32 [768], replicated
- grad_shift_two: float32 [768], replicated
- grad_clips: float32 [4], replicated
Inputs may be any that keep to these rules, and one draw needn't show every extreme that they name: `lengths`: live tokens of each row, at the start of the row; some row has all 512. `lat_qkv`: no entry is zero; within each matrix every magnitude lies within a factor of ten of the largest. `lat_out`: no entry is zero; within each matrix every magnitude lies within a factor of ten of the largest. `lat_up`: no entry is zero; within each matrix every magnitude lies within a factor of ten of the largest. `lat_down`: no entry is zero; within each matrix every magnitude lies within a factor of ten of the largest. `clips`: all four bounds are positive.
All inputs are finite; a program needn't handle non-finite values.
Results may differ from a plain program's by a relative error of at most 0.015.
The roundings to bfloat16 on the way count: a program that leaves them out, or rounds other values in their place, can miss the bound.
Values may be sent and summed in bfloat16 or wider, within the bound.
A program may use at most 320 MiB of HBM per device.

v0:
```python
import math

import jax
import jax.numpy as jnp
from jax import lax
from jax.sharding import PartitionSpec as P

D = 768
HEADS = 12
HEAD_DIM = 64
ROW = 512


EPSILON = 1e-05
MASKED = -1000000000.0


def binarize(latent):
    factor = jnp.mean(jnp.abs(latent), axis=1, keepdims=True)
    return (factor * jnp.sign(latent)).astype(jnp.bfloat16)


def normalize(value):
    center = value - jnp.mean(value, axis=-1, keepdims=True)
    spread = jnp.mean(center * center, axis=-1, keepdims=True)
    return center * lax.rsqrt(spread + EPSILON)


def norm_affine(value, gain_vec, shift_vec):
    return normalize(value) * gain_vec + shift_vec


def clipped(value, bound):
    return jnp.clip(value, -bound, bound)


def gelu_clipped(value, bound):
    return jnp.clip(jax.nn.gelu(value, approximate=False), -bound, bound)


def project(left, weight):
    return jnp.einsum("rtd,de->rte", left, weight, preferred_element_type=jnp.float32)


def back_project(grad_rows, weight):
    return jnp.einsum("rte,de->rtd", grad_rows, weight, preferred_element_type=jnp.float32)


def weight_grad(left, right):
    return jnp.einsum("rtd,rte->de", left, right, preferred_element_type=jnp.float32)


def heads_split(value):
    return value.reshape(value.shape[0], HEADS, HEAD_DIM)


def row_scores(queries, keys):
    raw = jnp.einsum(
        "qhe,khe->hqk", heads_split(queries), heads_split(keys), preferred_element_type=jnp.float32
    )
    return raw * (1.0 / math.sqrt(HEAD_DIM))


def row_attention(slab):
    queries, keys, values, live = slab
    key_live = live[None, None, :]
    masked = jnp.where(key_live, row_scores(queries, keys), MASKED)
    top = jnp.max(masked, axis=-1, keepdims=True)
    expo = jnp.exp(masked - top)
    total = jnp.sum(expo, axis=-1, keepdims=True)
    probs = (expo / total).astype(jnp.bfloat16)
    context = jnp.einsum(
        "hqk,khe->qhe", probs, heads_split(values), preferred_element_type=jnp.float32
    )
    return (context.reshape(queries.shape), top + jnp.log(total))


def row_backward(slab):
    queries, keys, values, t_queries, t_keys, log_total, d_context, live = slab
    key_live = live[None, None, :]
    pair = jnp.logical_and(live[None, :, None], key_live)
    raw = row_scores(queries, keys)
    probs = jnp.exp(jnp.where(key_live, raw, MASKED) - log_total)
    d_heads = heads_split(d_context)
    d_probs = jnp.einsum(
        "qhe,khe->hqk", d_heads, heads_split(values), preferred_element_type=jnp.float32
    )
    d_values = jnp.einsum(
        "hqk,qhe->khe", probs.astype(jnp.bfloat16), d_heads, preferred_element_type=jnp.float32
    )
    row_dot = jnp.sum(d_probs * probs, axis=-1, keepdims=True)
    score_gap = raw - row_scores(t_queries, t_keys)
    d_raw = (probs * (d_probs - row_dot) + jnp.where(pair, score_gap, 0.0) / ROW).astype(
        jnp.bfloat16
    )
    factor = 1.0 / math.sqrt(HEAD_DIM)
    d_queries = (
        jnp.einsum("hqk,khe->qhe", d_raw, heads_split(keys), preferred_element_type=jnp.float32)
        * factor
    )
    d_keys = (
        jnp.einsum("hqk,qhe->khe", d_raw, heads_split(queries), preferred_element_type=jnp.float32)
        * factor
    )
    width = queries.shape
    return (
        d_queries.reshape(width).astype(jnp.bfloat16),
        d_keys.reshape(width).astype(jnp.bfloat16),
        d_values.reshape(width).astype(jnp.bfloat16),
    )


def on_device(
    hidden,
    teacher_input,
    cotangent,
    lengths,
    lat_qkv,
    lat_out,
    lat_up,
    lat_down,
    bias_q,
    bias_v,
    bias_out,
    bias_up,
    bias_down,
    gain_one,
    shift_one,
    gain_two,
    shift_two,
    clips,
    teach_qkv,
    teach_out,
    teach_up,
    teach_down,
):
    w_qkv, w_out, w_up, w_down = (
        lax.all_gather(binarize(lat_qkv), "shard", axis=0, tiled=True),
        lax.all_gather(binarize(lat_out), "shard", axis=0, tiled=True),
        lax.all_gather(binarize(lat_up), "shard", axis=0, tiled=True),
        lax.all_gather(binarize(lat_down), "shard", axis=0, tiled=True),
    )
    t_qkv, t_out, t_up, t_down = (
        lax.all_gather(teach_qkv, "shard", axis=0, tiled=True),
        lax.all_gather(teach_out, "shard", axis=0, tiled=True),
        lax.all_gather(teach_up, "shard", axis=0, tiled=True),
        lax.all_gather(teach_down, "shard", axis=0, tiled=True),
    )
    positions = jnp.arange(ROW, dtype=jnp.int32)
    live = positions[None, :] < lengths[:, None]
    live_f = live.astype(jnp.float32)
    t_joined = project(teacher_input, t_qkv)
    t_queries = t_joined[..., :D].astype(jnp.bfloat16)
    t_keys = t_joined[..., D : 2 * D].astype(jnp.bfloat16)
    t_values = t_joined[..., 2 * D :].astype(jnp.bfloat16)
    t_context, unused_total = lax.map(row_attention, (t_queries, t_keys, t_values, live))
    t_first = normalize(
        teacher_input.astype(jnp.float32) + project(t_context.astype(jnp.bfloat16), t_out)
    )
    t_inner = project(t_first.astype(jnp.bfloat16), t_up)
    t_final = normalize(
        t_first + project(jax.nn.gelu(t_inner, approximate=False).astype(jnp.bfloat16), t_down)
    )
    x_in = hidden.astype(jnp.float32)
    a_in = clipped(x_in, clips[0]).astype(jnp.bfloat16)
    joined = project(a_in, w_qkv)
    queries = (joined[..., :D] + bias_q).astype(jnp.bfloat16)
    keys = joined[..., D : 2 * D].astype(jnp.bfloat16)
    values = (joined[..., 2 * D :] + bias_v).astype(jnp.bfloat16)
    context, log_total = lax.map(row_attention, (queries, keys, values, live))
    cut = clipped(context, clips[1]).astype(jnp.bfloat16)
    res_one = x_in + project(cut, w_out) + bias_out
    h_one = norm_affine(res_one, gain_one, shift_one)
    up_in = clipped(h_one, clips[2]).astype(jnp.bfloat16)
    pre = project(up_in, w_up) + bias_up
    act = gelu_clipped(pre, clips[3]).astype(jnp.bfloat16)
    res_two = h_one + project(act, w_down) + bias_down
    out = norm_affine(res_two, gain_two, shift_two)
    d_out = (cotangent.astype(jnp.float32) + out - t_final) * live_f[..., None]
    unused_two, norm_two_back = jax.vjp(norm_affine, res_two, gain_two, shift_two)
    d_res_two, g_gain_two, g_shift_two = norm_two_back(d_out)
    d_down = d_res_two.astype(jnp.bfloat16)
    g_w_down = weight_grad(act, d_down)
    g_b_down = jnp.sum(d_down.astype(jnp.float32), axis=(0, 1))
    d_act = back_project(d_down, w_down)
    unused_act, act_back = jax.vjp(gelu_clipped, pre, clips[3])
    d_pre_full, g_clip_three = act_back(d_act)
    d_pre = d_pre_full.astype(jnp.bfloat16)
    g_w_up = weight_grad(up_in, d_pre)
    g_b_up = jnp.sum(d_pre.astype(jnp.float32), axis=(0, 1))
    d_up_in = back_project(d_pre, w_up)
    unused_cut, h_back = jax.vjp(clipped, h_one, clips[2])
    d_h_part, g_clip_two = h_back(d_up_in)
    unused_one, norm_one_back = jax.vjp(norm_affine, res_one, gain_one, shift_one)
    d_res_one, g_gain_one, g_shift_one = norm_one_back(d_res_two + d_h_part)
    d_attn = d_res_one.astype(jnp.bfloat16)
    g_w_out = weight_grad(cut, d_attn)
    g_b_out = jnp.sum(d_attn.astype(jnp.float32), axis=(0, 1))
    d_cut = back_project(d_attn, w_out)
    unused_ctx, ctx_back = jax.vjp(clipped, context, clips[1])
    d_context, g_clip_one = ctx_back(d_cut)
    d_queries, d_keys, d_values = lax.map(
        row_backward,
        (queries, keys, values, t_queries, t_keys, log_total, d_context.astype(jnp.bfloat16), live),
    )
    d_joined = jnp.concatenate([d_queries, d_keys, d_values], axis=-1)
    g_w_qkv = weight_grad(a_in, d_joined)
    g_b_q = jnp.sum(d_queries.astype(jnp.float32), axis=(0, 1))
    g_b_v = jnp.sum(d_values.astype(jnp.float32), axis=(0, 1))
    d_a_in = back_project(d_joined, w_qkv)
    unused_in, in_back = jax.vjp(clipped, x_in, clips[0])
    d_x_part, g_clip_zero = in_back(d_a_in)
    input_grad = (d_res_one + d_x_part).astype(jnp.bfloat16)
    g_clips = jnp.stack([g_clip_zero, g_clip_one, g_clip_two, g_clip_three])
    grad_lat_qkv, grad_lat_out, grad_lat_up, grad_lat_down = (
        lax.psum_scatter(g_w_qkv, "shard", scatter_dimension=0, tiled=True),
        lax.psum_scatter(g_w_out, "shard", scatter_dimension=0, tiled=True),
        lax.psum_scatter(g_w_up, "shard", scatter_dimension=0, tiled=True),
        lax.psum_scatter(g_w_down, "shard", scatter_dimension=0, tiled=True),
    )
    summed = lax.psum(
        (
            g_b_q,
            g_b_v,
            g_b_out,
            g_b_up,
            g_b_down,
            g_gain_one,
            g_shift_one,
            g_gain_two,
            g_shift_two,
            g_clips,
        ),
        "shard",
    )
    return (
        out.astype(jnp.bfloat16),
        input_grad,
        grad_lat_qkv,
        grad_lat_out,
        grad_lat_up,
        grad_lat_down,
        summed[0],
        summed[1],
        summed[2],
        summed[3],
        summed[4],
        summed[5],
        summed[6],
        summed[7],
        summed[8],
        summed[9],
    )


def solution(mesh):
    placed = (
        P("shard", None, None),
        P("shard", None, None),
        P("shard", None, None),
        P("shard"),
        P("shard", None),
        P("shard", None),
        P("shard", None),
        P("shard", None),
        P(),
        P(),
        P(),
        P(),
        P(),
        P(),
        P(),
        P(),
        P(),
        P(),
        P("shard", None),
        P("shard", None),
        P("shard", None),
        P("shard", None),
    )
    return jax.shard_map(
        on_device,
        mesh=mesh,
        in_specs=placed,
        out_specs=(
            P("shard", None, None),
            P("shard", None, None),
            P("shard", None),
            P("shard", None),
            P("shard", None),
            P("shard", None),
            P(),
            P(),
            P(),
            P(),
            P(),
            P(),
            P(),
            P(),
            P(),
            P(),
        ),
        check_vma=False,
    )
```

profile of v0, /device:TPU:0, one launch (start us, length us, event | category | flops | bytes accessed | tf_op | source)
XLA Modules:
  0.0 1308.8 jit_solution(9854942505973982382)
XLA Ops:
  26.7 47.0 %all-gather.17.cloned.1.call-done = bf16[768,2304]{1,0:T(8,128)(2,1)} async-done(((bf16[24,2304]{1,0:T(8,128)(2,1)}), bf16[768,2304]{1,0:T(8,128)(2,1)}) %all-gather.17.cloned.1.call-update) | async-done | bytes 3538960 | tf_op jit(solution)/shard_map/all_gather | solution.py:144
  91.9 67.7 %while.40 = (s32[]{:T(128)}, bf16[3,512,768]{1,2,0:T(8,128)(2,1)}, bf16[3,512,768]{2,1,0:T(8,128)(2,1)}, pred[3,512]{1,0:T(4,128)(4,1)S(1)}, bf16[3,512,768]{1,2,0:T(8,128)(2,1)S(1)}, /*index=5*/bf16[3,512,768]{1,2,0:T(8,128)(2,1)}) while((s32[]{:T(128)}, bf16[3,512,768]{1,2,0:T(8,128)(2,1)}, bf16[3,512,768]{2,1,0:T(8,128)(2,1)}, ...), condition=%wide.region_15.16_spmd.clone, body=%wide.region_12.15_spmd.sunk.clone | while | flops 824181248 | bytes 39372408 | solution.py:156
  169.2 22.8 %all-gather.9.cloned.1.call-done = bf16[768,2304]{1,0:T(8,128)(2,1)} async-done(((bf16[24,2304]{1,0:T(8,128)(2,1)}), bf16[768,2304]{1,0:T(8,128)(2,1)}) %all-gather.9.cloned.1.call-update) | async-done | bytes 3538960 | tf_op jit(solution)/shard_map/all_gather | solution.py:138
  216.5 37.6 %while.39 = (s32[]{:T(128)}, f32[3,512,768]{1,2,0:T(8,128)}, f32[3,12,512,1]{2,1,3,0:T(8,128)}, bf16[3,512,768]{1,2,0:T(8,128)(2,1)S(1)}, pred[3,512]{1,0:T(4,12...) while((s32[]{:T(128)}, f32[3,512,768]{1,2,0:T(8,128)}, ...), condition=%wide.region_4.5_spmd.clone, body=%wide.region_1.4_spmd.sunk.clone | while | flops 843048960 | bytes 49752680 | solution.py:170
  271.1 42.5 %all-gather.21.cloned.1.call-done = bf16[768,3072]{1,0:T(8,128)(2,1)} async-done(((bf16[24,3072]{1,0:T(8,128)(2,1)}), bf16[768,3072]{1,0:T(8,128)(2,1)}) %all-gather.21.cloned.1.call-update) | async-done | bytes 4718608 | tf_op jit(solution)/shard_map/all_gather | solution.py:146
  313.6 21.3 %fusion.125 = (u8[512,3072]{1,0:T(8,128)(4,1)}, u8[512,3072]{1,0:T(8,128)(4,1)}, f32[3,512,3072]{2,1,0:T(8,128)}) fusion(bf16[768,3072]{1,0:T(8,128)(2,1)} %all-gather.21.cloned.1.call-done, f32[3,512,768]{2,1,0:T(8,128)} %copy-done.10, f32[3,512]{1,0:T(4,128)S(1)} %copy-done.33, f32[3,512]{1,0:T(4,128)S(1)} %copy-done.22), kind=kOutput, calls=%fused_computation.220 | convolution fusion | flops 7309492224 | bytes 31469568 | tf_op jit(solution)/shard_map/rtd,de->rte/dot_general | solution.py:42
  334.9 44.5 %all-gather.13.cloned.1.call-done = bf16[768,3072]{1,0:T(8,128)(2,1)} async-done(((bf16[24,3072]{1,0:T(8,128)(2,1)}), bf16[768,3072]{1,0:T(8,128)(2,1)}) %all-gather.13.cloned.1.call-update) | async-done | bytes 4718608 | tf_op jit(solution)/shard_map/all_gather | solution.py:140
  379.4 80.0 %fusion.95 = (u8[512,3072]{1,0:T(8,128)(4,1)}, u8[512,3072]{1,0:T(8,128)(4,1)}, u8[512,3072]{1,0:T(8,128)(4,1)}, u8[512,3072]{1,0:T(8,128)(4,1)}, u8[512,3072]{1...) fusion(f32[]{:T(128)S(6)} %neg.47, f32[]{:T(128)} %bitcast.28, ...), kind=kOutput, calls=%fused_computation.156 | convolution fusion | flops 7701921792 | bytes 75528208 | tf_op jit(solution)/shard_map/rtd,de->rte/dot_general | solution.py:42
  459.4 54.1 %fusion.197 = (f32[3,512]{1,0:T(4,128)S(1)}, f32[3,512,768]{2,1,0:T(8,128)S(1)}) fusion(bf16[3072,768]{1,0:T(8,128)(2,1)} %all-gather.23.cloned.1.call-done, f32[3,512,3072]{2,1,0:T(8,128)} %get-tuple-element.330, u8[512,3072]{1,0:T(8,128)(4,1)} %get-tuple-element.214, u8[512,3072]{1,0:T(8,128)(4,1)S(1)} %copy-done.51, f32[3,512]{1,0:T(4,128)S(1)} %copy-done.34, ...), kind=kOutput, calls=%fused_computation.311 | convolution fusion | flops 7582775808 | bytes 36194304 | tf_op jit(solution)/shard_map/rtd,de->rte/dot_general | solution.py:42
  545.2 42.3 %multiply_reduce_fusion.1 = (f32[]{:T(128)}, f32[]{:T(128)}, f32[3072]{0:T(1024)}, bf16[3,512,3072]{2,1,0:T(8,128)(2,1)}) fusion(u8[512,3072]{1,0:T(8,128)(4,1)} %get-tuple-element.212, u8[512,3072]{1,0:T(8,128)(4,1)} %get-tuple-element.207, u8[512,3072]{1,0:T(8,128)(4,1)} %get-tuple-element.209, u8[512,3072]{1,0:T(8,128)(4,1)} %get-tuple-element.208, ...), kind=kOutput, calls=%fused_computation.102 | convolution fusion | flops 7493121024 | bytes 82599952 | tf_op jit(solution)/shard_map/rte,de->rtd/dot_general | solution.py:46
  587.4 19.4 %multiply_reduce_fusion.4 = (f32[768]{0:T(1024)}, f32[3,512]{1,0:T(4,128)S(1)}, f32[]{:T(128)}, f32[]{:T(128)}, f32[768]{0:T(1024)}, /*index=5*/f32[3,512,768]{2,1,0:T(8,128)S(1)}) fusion(f32[3,512,768]{2,1,0:T(8,128)} %copy-done.5, f32[3,512]{1,0:T(4,128)S(1)} %fusion.152, f32[3,512]{1,0:T(4,128)S(1)} %broadcast_multiply_fusion.3, ...), kind=kOutput, calls=%fused_computation.197 | convolution fusion | flops 7289041920 | bytes 28348432 | tf_op jit(solution)/shard_map/rte,de->rtd/dot_general | solution.py:46
  626.9 252.4 %while.41 = (s32[]{:T(128)}, bf16[3,512,768]{1,2,0:T(8,128)(2,1)}, bf16[3,512,768]{2,1,0:T(8,128)(2,1)}, bf16[3,512,768]{1,2,0:T(8,128)(2,1)}, bf16[3,512,768]{1...) while((s32[]{:T(128)}, bf16[3,512,768]{1,2,0:T(8,128)(2,1)}, ...), condition=%wide.region_26.28_spmd.clone, body=%wide.region_24.27_spmd.sunk.clone | while | flops 2525115392 | bytes 203812016 | solution.py:202
  653.9 27.4 %multiply_convert_fusion.12 = bf16[12,64,512]{2,1,0:T(8,128)(2,1)S(1)} fusion(bf16[512,12,64]{0,2,1:T(8,128)(2,1)S(1)} %bitcast.235, f32[12,512,512]{1,2,0:T(8,128)} %fusion.307, f32[12,512,512]{1,2,0:T(8,128)} %fusion.308, f32[12,512,512]{1,2,0:T(8,128)} %copy-done, f32[12,512]{1,0:T(8,128)S(1)} %dynamic-slice_bitcast_fusion.3, ...), kind=kOutput, calls=%fused_computation.55.clone.1.clone | convolution fusion | flops 450632192 | bytes 39608832 | tf_op jit(solution)/shard_map/while/body/eval_jaxpr/hqk,khe->qhe/dot_general | solution.py:98
  682.6 27.3 %multiply_convert_fusion.13 = bf16[12,64,512]{2,1,0:T(8,128)(2,1)S(1)} fusion(bf16[512,12,64]{0,2,1:T(8,128)(2,1)S(1)} %bitcast.233, f32[12,512,512]{1,2,0:T(8,128)} %fusion.307, f32[12,512,512]{1,2,0:T(8,128)} %fusion.308, f32[12,512,512]{1,2,0:T(8,128)} %copy-done, f32[12,512]{1,0:T(8,128)S(1)} %dynamic-slice_bitcast_fusion.3, ...), kind=kOutput, calls=%fused_computation.54.clone.1.clone | convolution fusion | flops 450632192 | bytes 39608832 | tf_op jit(solution)/shard_map/while/body/eval_jaxpr/hqk,qhe->khe/dot_general | solution.py:102
  737.9 27.3 %multiply_convert_fusion.12 = bf16[12,64,512]{2,1,0:T(8,128)(2,1)S(1)} fusion(bf16[512,12,64]{0,2,1:T(8,128)(2,1)S(1)} %bitcast.235, f32[12,512,512]{1,2,0:T(8,128)} %fusion.307, f32[12,512,512]{1,2,0:T(8,128)} %fusion.308, f32[12,512,512]{1,2,0:T(8,128)} %copy-done, f32[12,512]{1,0:T(8,128)S(1)} %dynamic-slice_bitcast_fusion.3, ...), kind=kOutput, calls=%fused_computation.55.clone.1.clone | convolution fusion | flops 450632192 | bytes 39608832 | tf_op jit(solution)/shard_map/while/body/eval_jaxpr/hqk,khe->qhe/dot_general | solution.py:98
  766.5 27.3 %multiply_convert_fusion.13 = bf16[12,64,512]{2,1,0:T(8,128)(2,1)S(1)} fusion(bf16[512,12,64]{0,2,1:T(8,128)(2,1)S(1)} %bitcast.233, f32[12,512,512]{1,2,0:T(8,128)} %fusion.307, f32[12,512,512]{1,2,0:T(8,128)} %fusion.308, f32[12,512,512]{1,2,0:T(8,128)} %copy-done, f32[12,512]{1,0:T(8,128)S(1)} %dynamic-slice_bitcast_fusion.3, ...), kind=kOutput, calls=%fused_computation.54.clone.1.clone | convolution fusion | flops 450632192 | bytes 39608832 | tf_op jit(solution)/shard_map/while/body/eval_jaxpr/hqk,qhe->khe/dot_general | solution.py:102
  821.9 27.3 %multiply_convert_fusion.12 = bf16[12,64,512]{2,1,0:T(8,128)(2,1)S(1)} fusion(bf16[512,12,64]{0,2,1:T(8,128)(2,1)S(1)} %bitcast.235, f32[12,512,512]{1,2,0:T(8,128)} %fusion.307, f32[12,512,512]{1,2,0:T(8,128)} %fusion.308, f32[12,512,512]{1,2,0:T(8,128)} %copy-done, f32[12,512]{1,0:T(8,128)S(1)} %dynamic-slice_bitcast_fusion.3, ...), kind=kOutput, calls=%fused_computation.55.clone.1.clone | convolution fusion | flops 450632192 | bytes 39608832 | tf_op jit(solution)/shard_map/while/body/eval_jaxpr/hqk,khe->qhe/dot_general | solution.py:98
  850.5 27.3 %multiply_convert_fusion.13 = bf16[12,64,512]{2,1,0:T(8,128)(2,1)S(1)} fusion(bf16[512,12,64]{0,2,1:T(8,128)(2,1)S(1)} %bitcast.233, f32[12,512,512]{1,2,0:T(8,128)} %fusion.307, f32[12,512,512]{1,2,0:T(8,128)} %fusion.308, f32[12,512,512]{1,2,0:T(8,128)} %copy-done, f32[12,512]{1,0:T(8,128)S(1)} %dynamic-slice_bitcast_fusion.3, ...), kind=kOutput, calls=%fused_computation.54.clone.1.clone | convolution fusion | flops 450632192 | bytes 39608832 | tf_op jit(solution)/shard_map/while/body/eval_jaxpr/hqk,qhe->khe/dot_general | solution.py:102
  915.4 15.8 %convolution_bitcast_fusion = f32[3072,768]{1,0:T(8,128)} fusion(bf16[3,512,768]{2,1,0:T(8,128)(2,1)} %copy-done.11, f32[3,512,3072]{2,1,0:T(8,128)} %get-tuple-element.298, f32[]{:T(128)S(6)} %neg.47, f32[]{:T(128)} %bitcast.28), kind=kOutput, calls=%fused_computation.151 | convolution fusion | flops 7271350272 | bytes 30670856 | tf_op jit(solution)/shard_map/rtd,rte->de/dot_general | solution.py:50
  933.2 15.7 %fusion.113 = (f32[]{:T(128)}, f32[]{:T(128)}, bf16[3,512,768]{2,1,0:T(8,128)(2,1)}) fusion(bf16[3,512,768]{2,1,0:T(8,128)(2,1)} %param.31, f32[]{:T(128)S(6)} %neg.46, f32[]{:T(128)} %bitcast.25, f32[3,512,768]{2,1,0:T(8,128)} %copy-done.6, f32[3,512]{1,0:T(4,128)S(1)} %copy-done.25, bf16[768,2304]{1,0:T(8,128)(2,1)} %all-gather.9.cloned.1.call-done, ...), kind=kOutput, calls=%fused_computation.181 | convolution fusion | flops 5488902144 | bytes 20060176 | tf_op jit(solution)/shard_map/rte,de->rtd/dot_general | solution.py:46
  954.9 41.9 %all-reduce = (f32[768]{0:T(1024)}, f32[768]{0:T(1024)}, f32[768]{0:T(1024)}, f32[3072]{0:T(1024)}, f32[768]{0:T(1024)}, /*index=5*/f32[768]{0:T(1024)}, f32[768...) all-reduce(f32[768]{0:T(1024)S(1)} %get-tuple-element.339, ...), channel_id=1, replica_groups=mesh['shard'=32] {'shard'}, use_global_device_ids=true, to_apply=%region_32.34 | all-reduce | flops 9220 | bytes 73760 | tf_op jit(solution)/shard_map/psum | solution.py:221
  996.8 21.5 %reduce-scatter.5.cloned.1.call-done = f32[24,2304]{1,0:T(8,128)} async-done(((f32[768,2304]{1,0:T(8,128)}), f32[24,2304]{1,0:T(8,128)}) %reduce-scatter.5.cloned.1.call-update) | async-done | bytes 221200 | tf_op jit(solution)/shard_map/reduce_scatter | solution.py:216
  1018.2 141.4 %reduce-scatter.9.cloned.1.call-done = f32[24,3072]{1,0:T(8,128)} async-done(((f32[768,3072]{1,0:T(8,128)}), f32[24,3072]{1,0:T(8,128)}) %reduce-scatter.9.cloned.1.call-update) | async-done | bytes 294928 | tf_op jit(solution)/shard_map/reduce_scatter | solution.py:218
  1159.6 141.9 %reduce-scatter.11.cloned.1.call-done = f32[96,768]{1,0:T(8,128)} async-done(((f32[3072,768]{1,0:T(8,128)}), f32[96,768]{1,0:T(8,128)}) %reduce-scatter.11.cloned.1.call-update) | async-done | bytes 294928 | tf_op jit(solution)/shard_map/reduce_scatter | solution.py:219
  (310 shorter events, 368.3 us)
Async XLA Ops:
  7.2 66.5 %copy-start.43 = (bf16[3,512,768]{2,1,0:T(8,128)(2,1)S(1)}, bf16[3,512,768]{2,1,0:T(8,128)(2,1)}, u32[]{:S(2)}) copy-start(bf16[3,512,768]{2,1,0:T(8,128)(2,1)} %param.32) | copy-start | bytes 7077892
  7.2 66.5 %all-gather.17.cloned.1.call-start = ((), (), s32[]{:S(2)}) async-start(), calls=%async_computation.8 | async-start | bytes 3649536 | tf_op jit(solution)/shard_map/all_gather | solution.py:144
  7.9 151.7 %all-gather.19.cloned.1.call-start = ((), (), s32[]{:S(2)}) async-start(), calls=%async_computation.9 | async-start | bytes 1216512 | tf_op jit(solution)/shard_map/all_gather | solution.py:145
  8.7 183.3 %all-gather.9.cloned.1.call-start = ((), (), s32[]{:S(2)}) async-start(), calls=%async_computation.4 | async-start | bytes 3649536 | tf_op jit(solution)/shard_map/all_gather | solution.py:138
  11.5 249.7 %all-gather.11.cloned.1.call-start = ((), (), s32[]{:S(2)}) async-start(), calls=%async_computation.5 | async-start | bytes 1216512 | tf_op jit(solution)/shard_map/all_gather | solution.py:139
  14.2 299.4 %all-gather.21.cloned.1.call-start = ((), (), s32[]{:S(2)}) async-start(), calls=%async_computation.10 | async-start | bytes 4866048 | tf_op jit(solution)/shard_map/all_gather | solution.py:146
  14.8 364.6 %all-gather.13.cloned.1.call-start = ((), (), s32[]{:S(2)}) async-start(), calls=%async_computation.6 | async-start | bytes 4866048 | tf_op jit(solution)/shard_map/all_gather | solution.py:140
  17.6 441.8 %all-gather.23.cloned.1.call-start = ((), (), s32[]{:S(2)}) async-start(), calls=%async_computation.11 | async-start | bytes 4866048 | tf_op jit(solution)/shard_map/all_gather | solution.py:147
  18.4 498.0 %all-gather.15.cloned.1.call-start = ((), (), s32[]{:S(2)}) async-start(), calls=%async_computation.7 | async-start | bytes 4866048 | tf_op jit(solution)/shard_map/all_gather | solution.py:141
  21.3 975.5 %reduce-scatter.7.cloned.1.call-start = ((), (), s32[]{:S(2)}) async-start(), calls=%async_computation.13 | async-start | bytes 2433024 | tf_op jit(solution)/shard_map/reduce_scatter | solution.py:217
  267.7 45.9 %copy-start.22 = (f32[3,512]{1,0:T(4,128)S(1)}, f32[3,512]{1,0:T(4,128)}, u32[]{:S(2)}) copy-start(f32[3,512]{1,0:T(4,128)} %copy-done.21) | copy-start | bytes 18436
  267.7 45.9 %copy-start.33 = (f32[3,512]{1,0:T(4,128)S(1)}, f32[3,512]{1,0:T(4,128)}, u32[]{:S(2)}) copy-start(f32[3,512]{1,0:T(4,128)} %add_rsqrt_fusion.1) | copy-start | bytes 18436
  267.7 339.2 %copy-start.14 = (f32[3,512]{1,0:T(4,128)}, f32[3,512]{1,0:T(4,128)S(1)}, u32[]{:S(2)}) copy-start(f32[3,512]{1,0:T(4,128)S(1)} %broadcast_multiply_fusion.3) | copy-start | bytes 18436
  271.1 335.8 %copy-start.19 = (f32[3,512]{1,0:T(4,128)}, f32[3,512]{1,0:T(4,128)S(1)}, u32[]{:S(2)}) copy-start(f32[3,512]{1,0:T(4,128)S(1)} %fusion.152) | copy-start | bytes 18436
  271.1 108.3 %copy-start.40 = (f32[768]{0:T(1024)S(1)}, f32[768]{0:T(1024)}, u32[]{:S(2)}) copy-start(f32[768]{0:T(1024)} %param.44) | copy-start | bytes 9220
  271.1 108.3 %copy-start.45 = (f32[3072]{0:T(1024)S(1)}, f32[3072]{0:T(1024)}, u32[]{:S(2)}) copy-start(f32[3072]{0:T(1024)} %param.42) | copy-start | bytes 36868
  271.1 108.3 %copy-start.49 = (f32[768]{0:T(1024)S(1)}, f32[768]{0:T(1024)}, u32[]{:S(2)}) copy-start(f32[768]{0:T(1024)} %param.45) | copy-start | bytes 9220
  379.4 80.0 %copy-start.23 = (f32[3,512]{1,0:T(4,128)S(1)}, f32[3,512]{1,0:T(4,128)}, u32[]{:S(2)}) copy-start(f32[3,512]{1,0:T(4,128)} %copy-done.21) | copy-start | bytes 18436
  379.4 80.0 %copy-start.34 = (f32[3,512]{1,0:T(4,128)S(1)}, f32[3,512]{1,0:T(4,128)}, u32[]{:S(2)}) copy-start(f32[3,512]{1,0:T(4,128)} %add_rsqrt_fusion.1) | copy-start | bytes 18436
  379.4 80.0 %copy-start.51 = (u8[512,3072]{1,0:T(8,128)(4,1)S(1)}, u8[512,3072]{1,0:T(8,128)(4,1)}, u32[]{:S(2)}) copy-start(u8[512,3072]{1,0:T(8,128)(4,1)} %get-tuple-element.213) | copy-start | bytes 4718596
  545.2 42.3 %copy-start.11 = (bf16[3,512,768]{2,1,0:T(8,128)(2,1)}, bf16[3,512,768]{2,1,0:T(8,128)(2,1)S(1)}, u32[]{:S(2)}) copy-start(bf16[3,512,768]{2,1,0:T(8,128)(2,1)S(1)} %get-tuple-element.290) | copy-start | bytes 7077892
  617.7 400.5 %reduce-scatter.5.cloned.1.call-start = ((), (), s32[]{:S(2)}) async-start(), calls=%async_computation.12 | async-start | bytes 7299072 | tf_op jit(solution)/shard_map/reduce_scatter | solution.py:216
  899.2 260.5 %reduce-scatter.9.cloned.1.call-start = ((), (), s32[]{:S(2)}) async-start(), calls=%async_computation.14 | async-start | bytes 9732096 | tf_op jit(solution)/shard_map/reduce_scatter | solution.py:218
  915.3 386.2 %reduce-scatter.11.cloned.1.call-start = ((), (), s32[]{:S(2)}) async-start(), calls=%async_computation.15 | async-start | bytes 9732096 | tf_op jit(solution)/shard_map/reduce_scatter | solution.py:219
  (48 other events, 290.7 us)
Sparse Core Ops, SparseCore 0:
  10.9 62.7 all-gather.16
  76.6 52.8 all-gather.18
  133.0 58.9 all-gather.8
  195.3 52.8 all-gather.10
  250.9 62.5 all-gather.20
  316.9 62.4 all-gather.12
  382.3 62.4 all-gather.22
  448.3 62.4 all-gather.14
  617.8 97.8 reduce-scatter.6
  899.3 118.8 reduce-scatter.4
  1024.7 134.8 reduce-scatter.8
  1166.9 134.5 reduce-scatter.10
where the time goes:
time: 1320 us; the launch traced here: 1310 us
  matrix products  620 us (47%)
  waiting for transfers between devices  464 us (35%)
  local copies, waits for them, and re-layouts  111 us (8%)
  other arithmetic  46.5 us (4%)
  blocking collectives  41.9 us (3%)
  between operations  23.2 us (2%)
    dot_general x8, matrix products, project(): jnp.einsum('rtd,de->rte', left, weight, preferred_element_type=jnp.float32)  199 us
    reduce_scatter x1, waiting for transfers between devices, on_device(): lax.psum_scatter(g_w_down, 'shard', scatter_dimension=0, tiled=True)  142 us
    reduce_scatter x1, waiting for transfers between devices, on_device(): lax.psum_scatter(g_w_up, 'shard', scatter_dimension=0, tiled=True)  141 us
    dot_general x4, matrix products, back_project(): jnp.einsum('rte,de->rtd', grad_rows, weight, preferred_element_type=jnp.f...  86.5 us
    dot_general x3, matrix products, row_backward(): jnp.einsum('hqk,qhe->khe', d_raw, heads_split(queries), preferred_element...  82 us
    dot_general x3, matrix products, row_backward(): jnp.einsum('hqk,khe->qhe', d_raw, heads_split(keys), preferred_element_ty...  82 us
    dot_general x4, matrix products, weight_grad(): jnp.einsum('rtd,rte->de', left, right, preferred_element_type=jnp.float32)  48.2 us
    all_gather x1, waiting for transfers between devices, on_device(): lax.all_gather(teach_qkv, 'shard', axis=0, tiled=True)  47 us
  transfers between devices with their start and end apart: 12, of which 7 were waited for; matrix products, arithmetic and copies ran while one was open for 51% of the time, Pallas kernels for 0%

commit v1 on v0

v1 whole, which is shorter than its diff:
```python
import functools
import math

import jax
import jax.numpy as jnp
from jax import lax
from jax.experimental import pallas as pl
from jax.experimental.pallas import tpu as pltpu
from jax.sharding import PartitionSpec as P

D = 768
FF = 3072
HEAD_DIM = 64
PAIR = 2 * HEAD_DIM
PAIRS = D // PAIR
CHUNKS = FF // D

EPSILON = 1e-05
MASKED = -1000000000.0
SCALE = 1.0 / math.sqrt(HEAD_DIM)

F32 = jnp.float32
BF16 = jnp.bfloat16
MESH = pl.DeviceIdType.MESH
VMEM_LIMIT = 60 * 1024 * 1024


def nn(left, right):
    return lax.dot_general(left, right, (((1,), (0,)), ((), ())), preferred_element_type=F32)


def nt(left, right):
    return lax.dot_general(left, right, (((1,), (1,)), ((), ())), preferred_element_type=F32)


def tn(left, right):
    return lax.dot_general(left, right, (((0,), (0,)), ((), ())), preferred_element_type=F32)


def signed_mean(latent):
    factor = jnp.mean(jnp.abs(latent), axis=1, keepdims=True)
    sign = jnp.where(latent > 0, 1.0, jnp.where(latent < 0, -1.0, 0.0))
    return (factor * sign).astype(BF16)


def normalize(value):
    center = value - jnp.mean(value, axis=-1, keepdims=True)
    inverse = lax.rsqrt(jnp.mean(center * center, axis=-1, keepdims=True) + EPSILON)
    return center * inverse, inverse


def norm_back(d_normed, normed, inverse):
    first = jnp.mean(d_normed, axis=-1, keepdims=True)
    second = jnp.mean(d_normed * normed, axis=-1, keepdims=True)
    return inverse * (d_normed - first - normed * second)


def normal_cdf(value):
    return 0.5 * (1.0 + lax.erf(value * (1.0 / math.sqrt(2.0))))


def column_sum(value):
    return jnp.sum(value, axis=0, keepdims=True)


def head_halves(pair):
    first = lax.broadcasted_iota(jnp.int32, pair.shape, 1) < HEAD_DIM
    zero = jnp.zeros_like(pair)
    return jnp.where(first, pair, zero), jnp.where(first, zero, pair)


def attend_pair(queries, keys, values, length):
    tokens = queries.shape[0]
    values_t = values.T
    key_live = lax.broadcasted_iota(jnp.int32, (tokens, tokens), 0) < length
    contexts, log_totals = [], []
    for head, one in enumerate(head_halves(queries)):
        masked = jnp.where(key_live, nt(keys, one), MASKED)
        top = jnp.max(masked, axis=0, keepdims=True)
        expo = jnp.exp(masked - top)
        total = jnp.sum(expo, axis=0, keepdims=True)
        probs = (expo * (1.0 / total)).astype(BF16)
        contexts.append(nn(values_t[HEAD_DIM * head : HEAD_DIM * (head + 1)], probs))
        log_totals.append(top + jnp.log(total))
    return jnp.concatenate(contexts, axis=0).T, jnp.concatenate(log_totals, axis=0)


def attend_pair_back(queries, keys, values, t_queries, t_keys, log_totals, d_context, length):
    tokens = queries.shape[0]
    shape = (tokens, tokens)
    key_live = lax.broadcasted_iota(jnp.int32, shape, 0) < length
    pair_live = jnp.logical_and(key_live, lax.broadcasted_iota(jnp.int32, shape, 1) < length)
    keys_t = keys.T
    d_queries, d_keys, d_values = [], [], []
    heads = zip(head_halves(queries), head_halves(d_context), head_halves(t_queries))
    for head, (one, d_one, t_one) in enumerate(heads):
        scores = nt(keys, one)
        score_gap = scores - nt(t_keys, t_one)
        probs = jnp.exp(jnp.where(key_live, scores, MASKED) - log_totals[head : head + 1])
        d_probs = nt(values, d_one)
        weighted = probs * d_probs
        row_dot = jnp.sum(weighted, axis=0, keepdims=True)
        d_values.append(nn(probs.astype(BF16), d_one))
        extra = jnp.where(pair_live, score_gap, 0.0) * (1.0 / tokens)
        d_scores = (weighted - probs * row_dot + extra).astype(BF16)
        d_keys.append(nn(d_scores, one))
        d_queries.append(nn(keys_t[HEAD_DIM * head : HEAD_DIM * (head + 1)], d_scores))
    d_q = (jnp.concatenate(d_queries, axis=0).T * SCALE).astype(BF16)
    return d_q, (d_keys[0] + d_keys[1]).astype(BF16), (d_values[0] + d_values[1]).astype(BF16)


def pair_columns(base, pair):
    return pl.ds(pl.multiple_of(base + pair * PAIR, PAIR), PAIR)


def teacher_kernel(lengths, x_ref, w_qkv, w_out, w_up, w_down, tqk_ref, final_ref, values, context):
    length = lengths[pl.program_id(0)]
    x = x_ref[0]
    tqk_ref[0, :, :D] = (nn(x, w_qkv[:, :D]).astype(BF16).astype(F32) * SCALE).astype(BF16)
    tqk_ref[0, :, D:] = nn(x, w_qkv[:, D : 2 * D]).astype(BF16)
    values[...] = nn(x, w_qkv[:, 2 * D :]).astype(BF16)

    @pl.loop(0, PAIRS)
    def _(pair):
        queries, keys = tqk_ref[0, :, pair_columns(0, pair)], tqk_ref[0, :, pair_columns(D, pair)]
        mixed, _ = attend_pair(queries, keys, values[:, pair_columns(0, pair)], length)
        context[:, pair_columns(0, pair)] = mixed.astype(BF16)

    first, _ = normalize(x.astype(F32) + nn(context[...], w_out[...]))
    first_low = first.astype(BF16)
    total = first
    for c in range(CHUNKS):
        inner = nn(first_low, w_up[:, D * c : D * (c + 1)])
        total = total + nn((inner * normal_cdf(inner)).astype(BF16), w_down[D * c : D * (c + 1), :])
    final_ref[0] = normalize(total)[0]


def student_attend_kernel(lengths, clips, x_ref, w_qkv, bias_q, bias_v, qkv_ref, context_ref, log_ref):
    length = lengths[pl.program_id(0)]
    bound = clips[0]
    a_in = jnp.clip(x_ref[0].astype(F32), -bound, bound).astype(BF16)
    queries = (nn(a_in, w_qkv[:, :D]) + bias_q[...]).astype(BF16)
    qkv_ref[0, :, :D] = (queries.astype(F32) * SCALE).astype(BF16)
    qkv_ref[0, :, D : 2 * D] = nn(a_in, w_qkv[:, D : 2 * D]).astype(BF16)
    qkv_ref[0, :, 2 * D :] = (nn(a_in, w_qkv[:, 2 * D :]) + bias_v[...]).astype(BF16)

    @pl.loop(0, PAIRS)
    def _(pair):
        queries, keys, values = (qkv_ref[0, :, pair_columns(D * i, pair)] for i in range(3))
        mixed, log_totals = attend_pair(queries, keys, values, length)
        context_ref[0, :, pair_columns(0, pair)] = mixed
        log_ref[0, pair] = log_totals


(S_OUT, S_UP, S_DOWN, S_GAIN_ONE, S_SHIFT_ONE, S_GAIN_TWO, S_SHIFT_TWO, S_CLIP_ONE, S_CLIP_TWO, S_CLIP_THREE) = (
    0, 1, 5, 6, 7, 8, 9, 10, 11, 12,
)
S_ROWS = 16
(Q_QUERY, Q_VALUE, Q_CLIP) = (0, 1, 2)
Q_ROWS = 8
ABOVE, BELOW = 4.0, -4.0


def student_middle_kernel(
    lengths, clips, x_ref, cotangent_ref, final_ref, context_ref, w_out, w_up, w_down, vectors,
    mixed_ref, act_ref, d_pre_ref, up_in_ref, d_down_ref, cut_ref, d_attn_ref, d_res_ref, d_context_ref, sums_ref,
    slope,
):
    block = x_ref.shape[1]
    row, part = pl.program_id(0), pl.program_id(1)
    length = lengths[row] - part * block

    @pl.when(jnp.logical_and(row == 0, part == 0))
    def _():
        sums_ref[...] = jnp.zeros_like(sums_ref)

    def add(at, value):
        sums_ref[at : at + 1] += value

    def vector(at):
        return vectors[at : at + 1]

    cut = jnp.clip(context_ref[0], -clips[1], clips[1]).astype(BF16)
    cut_ref[0] = cut
    normed_one, inverse_one = normalize(x_ref[0].astype(F32) + nn(cut, w_out[...]) + vector(S_OUT))
    h_one = normed_one * vector(S_GAIN_ONE) + vector(S_SHIFT_ONE)
    up_in = jnp.clip(h_one, -clips[2], clips[2]).astype(BF16)
    up_in_ref[0] = up_in
    total = h_one + vector(S_DOWN)
    for c in range(CHUNKS):
        columns = slice(D * c, D * (c + 1))
        pre = nn(up_in, w_up[:, columns]) + vector(S_UP + c)
        cdf = normal_cdf(pre)
        value = pre * cdf
        rise = cdf + pre * jnp.exp(-0.5 * pre * pre) * (1.0 / math.sqrt(2.0 * math.pi))
        rise = jnp.where(value > clips[3], ABOVE, jnp.where(value < -clips[3], BELOW, rise))
        slope[:, columns] = rise
        act = jnp.clip(value, -clips[3], clips[3]).astype(BF16)
        act_ref[0, :, columns] = act
        total = total + nn(act, w_down[columns, :])
    normed_two, inverse_two = normalize(total)
    out = normed_two * vector(S_GAIN_TWO) + vector(S_SHIFT_TWO)
    mixed_ref[0] = out.astype(BF16)
    live = lax.broadcasted_iota(jnp.int32, (block, 1), 0) < length
    d_out = jnp.where(live, cotangent_ref[0].astype(F32) + out - final_ref[0], 0.0)
    add(S_GAIN_TWO, column_sum(d_out * normed_two))
    add(S_SHIFT_TWO, column_sum(d_out))
    d_res_two = norm_back(d_out * vector(S_GAIN_TWO), normed_two, inverse_two)
    d_down = d_res_two.astype(BF16)
    d_down_ref[0] = d_down
    add(S_DOWN, column_sum(d_down.astype(F32)))
    d_up_in = jnp.zeros((block, D), F32)
    for c in range(CHUNKS):
        columns = slice(D * c, D * (c + 1))
        d_act = nt(d_down, w_down[columns, :])
        rise = slope[:, columns]
        above, below = rise > 2.0, rise < -2.0
        d_pre = jnp.where(jnp.logical_or(above, below), 0.0, rise * d_act).astype(BF16)
        d_pre_ref[0, :, columns] = d_pre
        add(S_CLIP_THREE, column_sum(jnp.where(above, d_act, jnp.where(below, -d_act, 0.0))))
        add(S_UP + c, column_sum(d_pre.astype(F32)))
        d_up_in = d_up_in + nt(d_pre, w_up[:, columns])
    above, below = h_one > clips[2], h_one < -clips[2]
    add(S_CLIP_TWO, column_sum(jnp.where(above, d_up_in, jnp.where(below, -d_up_in, 0.0))))
    d_h_one = d_res_two + jnp.where(jnp.abs(h_one) < clips[2], d_up_in, 0.0)
    add(S_GAIN_ONE, column_sum(d_h_one * normed_one))
    add(S_SHIFT_ONE, column_sum(d_h_one))
    d_res_one = norm_back(d_h_one * vector(S_GAIN_ONE), normed_one, inverse_one)
    d_res_ref[0] = d_res_one
    d_attn = d_res_one.astype(BF16)
    d_attn_ref[0] = d_attn
    add(S_OUT, column_sum(d_attn.astype(F32)))
    d_cut = nt(d_attn, w_out[...])
    context = context_ref[0]
    above, below = context > clips[1], context < -clips[1]
    add(S_CLIP_ONE, column_sum(jnp.where(above, d_cut, jnp.where(below, -d_cut, 0.0))))
    d_context_ref[0] = jnp.where(jnp.abs(context) < clips[1], d_cut, 0.0).astype(BF16)


def weight_grads_kernel(act, d_down, up_in, d_pre, cut, d_attn, g_down, g_up, g_out):
    g_down[...] = tn(act[...], d_down[...]).astype(BF16)
    g_up[...] = tn(up_in[...], d_pre[...]).astype(BF16)

    @pl.when(pl.program_id(0) == 0)
    def _():
        g_out[...] = tn(cut[...], d_attn[...]).astype(BF16)


def student_back_kernel(
    lengths, clips, x_ref, qkv_ref, tqk_ref, log_ref, d_context_ref, d_res_ref, w_qkv,
    input_ref, g_qkv, sums_ref, a_in, d_joined,
):
    row = pl.program_id(0)
    tokens = x_ref.shape[1]
    length = lengths[row]
    here = pl.ds(pl.multiple_of(row * tokens, tokens), tokens)

    @pl.when(row == 0)
    def _():
        sums_ref[...] = jnp.zeros_like(sums_ref)

    @pl.loop(0, PAIRS)
    def _(pair):
        queries, keys, values = (qkv_ref[0, :, pair_columns(D * i, pair)] for i in range(3))
        t_queries, t_keys = (tqk_ref[0, :, pair_columns(D * i, pair)] for i in range(2))
        d_context = d_context_ref[0, :, pair_columns(0, pair)]
        grads = attend_pair_back(queries, keys, values, t_queries, t_keys, log_ref[0, pair], d_context, length)
        for i in range(3):
            d_joined[here, pair_columns(D * i, pair)] = grads[i]

    bound = clips[0]
    x = x_ref[0].astype(F32)
    a_in[here, :] = jnp.clip(x, -bound, bound).astype(BF16)
    sums_ref[Q_QUERY : Q_QUERY + 1] += column_sum(d_joined[here, :D].astype(F32))
    sums_ref[Q_VALUE : Q_VALUE + 1] += column_sum(d_joined[here, 2 * D :].astype(F32))
    d_a = nt(d_joined[here, :], w_qkv[...])
    inside = jnp.where(jnp.abs(x) < bound, 1.0, jnp.where(jnp.abs(x) == bound, 0.5, 0.0))
    input_ref[0] = (d_res_ref[0] + d_a * inside).astype(BF16)
    outside = (1.0 - inside) * d_a
    sums_ref[Q_CLIP : Q_CLIP + 1] += column_sum(jnp.where(x > 0, outside, -outside))

    @pl.when(row == pl.num_programs(0) - 1)
    def _():
        for i in range(3):
            g_qkv[:, D * i : D * (i + 1)] = tn(a_in[...], d_joined[:, D * i : D * (i + 1)]).astype(BF16)


def rows_spec(tokens, width):
    return pl.BlockSpec((1, tokens, width), lambda r, *_: (r, 0, 0))


def whole_spec(shape):
    return pl.BlockSpec(shape, lambda *_: (0,) * len(shape), pipeline_mode=pl.Buffered(1))


def smem_spec():
    return pl.BlockSpec(memory_space=pltpu.SMEM)


def params(**more):
    return pltpu.CompilerParams(vmem_limit_bytes=VMEM_LIMIT, **more)


def shaped(shape, dtype):
    return jax.ShapeDtypeStruct(shape, dtype)


def teacher_pass(lengths, x, w_qkv, w_out, w_up, w_down):
    rows, tokens, _ = x.shape
    return pl.pallas_call(
        teacher_kernel,
        grid=(rows,),
        in_specs=[smem_spec(), rows_spec(tokens, D)] + [whole_spec(w.shape) for w in (w_qkv, w_out, w_up, w_down)],
        out_specs=[rows_spec(tokens, 2 * D), rows_spec(tokens, D)],
        out_shape=[shaped((rows, tokens, 2 * D), BF16), shaped((rows, tokens, D), F32)],
        scratch_shapes=[pltpu.VMEM((tokens, D), BF16)] * 2,
        compiler_params=params(),
    )(lengths, x, w_qkv, w_out, w_up, w_down)


def student_attend(lengths, clips, x, w_qkv, bias_q, bias_v):
    rows, tokens, _ = x.shape
    logs = (1, PAIRS, 2, tokens)
    return pl.pallas_call(
        student_attend_kernel,
        grid=(rows,),
        in_specs=[smem_spec(), smem_spec(), rows_spec(tokens, D), whole_spec(w_qkv.shape)] + [whole_spec((1, D))] * 2,
        out_specs=[
            rows_spec(tokens, 3 * D),
            rows_spec(tokens, D),
            pl.BlockSpec(logs, lambda r: (r, 0, 0, 0)),
        ],
        out_shape=[
            shaped((rows, tokens, 3 * D), BF16),
            shaped((rows, tokens, D), F32),
            shaped((rows,) + logs[1:], F32),
        ],
        compiler_params=params(),
    )(lengths, clips, x, w_qkv, bias_q.reshape(1, D), bias_v.reshape(1, D))


def student_middle(lengths, clips, x, cotangent, final, context, w_out, w_up, w_down, vectors):
    rows, tokens, _ = x.shape
    block = tokens // 2 if tokens % 32 == 0 else tokens
    wide = {"act": FF, "d_pre": FF}
    names = ("mixed", "act", "d_pre", "up_in", "d_down", "cut", "d_attn", "d_res", "d_context")

    def spec(width):
        return pl.BlockSpec((1, block, width), lambda r, i: (r, i, 0))

    return pl.pallas_call(
        student_middle_kernel,
        grid=(rows, tokens // block),
        in_specs=[smem_spec(), smem_spec()]
        + [spec(D)] * 4
        + [whole_spec(w.shape) for w in (w_out, w_up, w_down, vectors)],
        out_specs=[spec(wide.get(name, D)) for name in names] + [whole_spec((S_ROWS, D))],
        out_shape=[
            shaped((rows, tokens, wide.get(name, D)), F32 if name == "d_res" else BF16) for name in names
        ]
        + [shaped((S_ROWS, D), F32)],
        scratch_shapes=[pltpu.VMEM((block, FF), F32)],
        compiler_params=params(),
    )(lengths, clips, x, cotangent, final, context, w_out, w_up, w_down, vectors)


def weight_grads(act, d_down, up_in, d_pre, cut, d_attn):
    flat = [v.reshape(-1, v.shape[-1]) for v in (act, d_down, up_in, d_pre, cut, d_attn)]
    tokens = flat[0].shape[0]
    chunk = pl.BlockSpec((tokens, D), lambda c: (0, c))
    same = whole_spec((tokens, D))
    return pl.pallas_call(
        weight_grads_kernel,
        grid=(CHUNKS,),
        in_specs=[chunk, same, same, chunk, same, same],
        out_specs=[
            pl.BlockSpec((D, D), lambda c: (c, 0)),
            pl.BlockSpec((D, D), lambda c: (0, c)),
            whole_spec((D, D)),
        ],
        out_shape=[shaped((FF, D), BF16), shaped((D, FF), BF16), shaped((D, D), BF16)],
        compiler_params=params(),
    )(*flat)


def student_back(lengths, clips, x, qkv, tqk, logs, d_context, d_res, w_qkv):
    rows, tokens, _ = x.shape
    return pl.pallas_call(
        student_back_kernel,
        grid=(rows,),
        in_specs=[smem_spec(), smem_spec(), rows_spec(tokens, D), rows_spec(tokens, 3 * D), rows_spec(tokens, 2 * D)]
        + [pl.BlockSpec((1,) + logs.shape[1:], lambda r: (r, 0, 0, 0))]
        + [rows_spec(tokens, D), rows_spec(tokens, D), whole_spec(w_qkv.shape)],
        out_specs=[rows_spec(tokens, D), whole_spec((D, 3 * D)), whole_spec((Q_ROWS, D))],
        out_shape=[shaped((rows, tokens, D), BF16), shaped((D, 3 * D), BF16), shaped((Q_ROWS, D), F32)],
        scratch_shapes=[pltpu.VMEM((rows * tokens, D), BF16), pltpu.VMEM((rows * tokens, 3 * D), BF16)],
        compiler_params=params(),
    )(lengths, clips, x, qkv, tqk, logs, d_context, d_res, w_qkv)


PLANES, COLUMNS, CORES = 4, 4, 2
DEVICES = PLANES * COLUMNS * CORES


class Place:
    def __init__(self):
        self.me = lax.axis_index("shard")
        self.core = self.me % 2
        self.x = (self.me // 2) % 2
        self.y = (self.me // 4) % 2
        self.z = self.me // 8
        self.column = (self.me // 2) % 4
        self.along_x = self.me + 2 - 4 * self.x
        self.along_y = self.me + 4 - 8 * self.y
        self.sibling = self.me + 1 - 2 * self.core
        self.along_a = self.along_x + (self.along_y - self.along_x) * self.core
        self.along_b = self.along_y + (self.along_x - self.along_y) * self.core

    def plane(self, step):
        return (self.me + 8 * step) % DEVICES

    def meet(self):
        partners = [self.sibling, self.along_x, self.along_y] + [self.plane(k) for k in range(1, PLANES)]
        barrier = pltpu.get_barrier_semaphore()
        for partner in partners:
            pl.semaphore_signal(barrier, inc=1, device_id=(partner,), device_id_type=MESH)
        pl.semaphore_wait(barrier, len(partners))


class Trip:
    SEMAPHORES = 12

    def __init__(self, place, source, out, send, receive):
        self.place, self.source, self.out, self.send, self.receive = place, source, out, send, receive
        self.mine = place.me % 8
        self.at_a = self.mine + place.along_a - place.me
        self.at_b = self.mine + place.along_b - place.me
        self.at_ab = self.at_a + self.at_b - self.mine

    def remote(self, source, target, slot, device):
        return pltpu.make_async_remote_copy(
            src_ref=source, dst_ref=target, send_sem=self.send.at[slot], recv_sem=self.receive.at[slot],
            device_id=(device,), device_id_type=MESH,
        )

    def own(self):
        return pltpu.make_async_copy(self.source, self.out.at[self.place.z, self.mine], self.send.at[0])

    def line(self, step):
        target = self.out.at[self.place.z, self.mine]
        return self.remote(self.source, target, step, self.place.plane(step))

    def line_from(self, step):
        target = self.out.at[(self.place.z + PLANES - step) % PLANES, self.mine]
        return self.remote(self.source, target, step, self.place.plane(step))

    def slab(self, column, slot, device):
        part = self.out.at[:, column]
        return self.remote(part, part, slot, device)

    def first(self):
        self.own().start()
        for step in range(1, PLANES):
            self.line(step).start()

    def second(self):
        place = self.place
        self.own().wait()
        for step in range(1, PLANES):
            self.line_from(step).wait_recv()
        self.slab(self.mine, 4, place.along_a).start()
        self.slab(self.mine, 5, place.along_b).start()
        self.slab(self.mine, 7, place.sibling).start()

    def third(self):
        place = self.place
        self.slab(self.at_a, 4, place.along_a).wait_recv()
        self.slab(self.at_a, 6, place.along_b).start()
        self.slab(self.at_a, 8, place.sibling).start()

    def fourth(self):
        place = self.place
        self.slab(self.at_b, 5, place.along_b).wait_recv()
        self.slab(self.at_b, 9, place.sibling).start()
        self.slab(self.at_ab, 6, place.along_b).wait_recv()
        self.slab(self.at_ab, 10, place.sibling).start()

    def fifth(self):
        for slot in range(7, 11):
            self.slab(self.mine, slot, self.place.sibling).wait_recv()

    def last(self):
        for step in range(1, PLANES):
            self.line(step).wait_send()
        for slot in range(4, 11):
            self.slab(self.mine, slot, self.place.sibling).wait_send()


def gather_kernel(*refs):
    teach, latent, outs, low = refs[:4], refs[4:8], refs[8:16], refs[16:20]
    send, receive = refs[20:]
    place = Place()
    place.meet()
    sources = list(teach) + list(low)
    trips = [Trip(place, source, outs[i], send.at[i], receive.at[i]) for i, source in enumerate(sources)]
    order = trips
    steps = [[t.first, t.second, t.third, t.fourth, t.fifth] for t in order]
    depth = len(steps[0])
    for tick in range(len(order) + depth - 1):
        for phase in reversed(range(depth)):
            if 0 <= tick - phase < len(order):
                steps[tick - phase][phase]()
        if tick == 0:
            for i in range(4):
                low[i][...] = signed_mean(latent[i][...])
    for trip in trips:
        trip.last()


def gather_weights(teach, latent):
    shapes = [(PLANES, 8) + w.shape for w in teach] * 2
    outs = pl.pallas_call(
        gather_kernel,
        in_specs=[pl.BlockSpec(memory_space=pl.ANY)] * 4 + [pl.BlockSpec(memory_space=pltpu.VMEM)] * 4,
        out_specs=[pl.BlockSpec(memory_space=pl.ANY)] * 8,
        out_shape=[shaped(shape, BF16) for shape in shapes],
        scratch_shapes=[pltpu.VMEM(w.shape, BF16) for w in latent]
        + [pltpu.SemaphoreType.DMA((8, Trip.SEMAPHORES))] * 2,
        compiler_params=params(collective_id=0, has_side_effects=True),
    )(*teach, *latent)
    whole = [out.reshape(-1, out.shape[-1]) for out in outs]
    return whole[:4], whole[4:]


class Fold:
    SEMAPHORES = 8

    def __init__(self, place, grad, out, own, from_core, to_p, from_p, to_q, from_q, to_z, from_z, send, receive):
        self.place, self.grad, self.out = place, grad, out
        self.own, self.from_core = own, from_core
        self.to_p, self.from_p, self.to_q, self.from_q = to_p, from_p, to_q, from_q
        self.to_z, self.from_z = to_z, from_z
        self.send, self.receive = send, receive
        core = place.core
        self.p_stride, self.q_stride = 1 + core, 2 - core
        self.p = place.x + (place.y - place.x) * core
        self.q = place.y + (place.x - place.y) * core

    def remote(self, source, target, slot, device):
        return pltpu.make_async_remote_copy(
            src_ref=source, dst_ref=target, send_sem=self.send.at[slot], recv_sem=self.receive.at[slot],
            device_id=(device,), device_id_type=MESH,
        )

    def column(self, p, q):
        return p * self.p_stride + q * self.q_stride

    def keep(self):
        return pltpu.make_async_copy(self.grad.at[:, :, self.place.core], self.own, self.send.at[0])

    def over_core(self):
        return self.remote(self.grad.at[:, :, 1 - self.place.core], self.from_core, 1, self.place.sibling)

    def over_p(self):
        return self.remote(self.to_p, self.from_p, 2, self.place.along_a)

    def over_q(self):
        return self.remote(self.to_q, self.from_q, 3, self.place.along_b)

    def over_z(self, step):
        return self.remote(self.to_z.at[step - 1], self.from_z.at[step - 1], 3 + step, self.place.plane(step))

    def pair_sum(self, z, column):
        return self.own[z, column].astype(F32) + self.from_core[z, column].astype(F32)

    def first(self):
        self.keep().start()
        self.over_core().start()

    def second(self):
        self.keep().wait()
        self.over_core().wait_recv()

        @pl.loop(0, 2 * PLANES)
        def _(i):
            z, q = i // 2, i % 2
            self.to_p[z, q] = self.pair_sum(z, self.column(1 - self.p, q)).astype(BF16)

        self.over_p().start()

    def third(self):
        self.over_p().wait_recv()

        @pl.loop(0, PLANES)
        def _(z):
            q = 1 - self.q
            total = self.pair_sum(z, self.column(self.p, q)) + self.from_p[z, q].astype(F32)
            self.to_q[z] = total.astype(BF16)

        self.over_q().start()

    def quad_sum(self, z):
        q = self.q
        total = self.pair_sum(z, self.column(self.p, q)) + self.from_p[z, q].astype(F32)
        return total + self.from_q[z].astype(F32)

    def fourth(self):
        self.over_q().wait_recv()
        for step in range(1, PLANES):
            self.to_z[step - 1] = self.quad_sum((self.place.z + step) % PLANES).astype(BF16)
            self.over_z(step).start()

    def fifth(self):
        total = self.quad_sum(self.place.z)
        for step in range(1, PLANES):
            self.over_z(step).wait_recv()
            total = total + self.from_z[step - 1].astype(F32)
        self.out[...] = total

    def last(self):
        self.over_core().wait_send()
        self.over_p().wait_send()
        self.over_q().wait_send()
        for step in range(1, PLANES):
            self.over_z(step).wait_send()


FOLD_BUFFERS = ((4, 4), (4, 4), (4, 2), (4, 2), (4,), (4,), (3,), (3,))


class Share:
    SEMAPHORES = 7

    def __init__(self, place, value, out, partial, received, send, receive):
        self.place, self.value, self.out = place, value, out
        self.partial, self.received, self.send, self.receive = partial, received, send, receive

    def swap(self, slot, device):
        return pltpu.make_async_remote_copy(
            src_ref=self.partial.at[min(slot, 3)], dst_ref=self.received.at[slot], send_sem=self.send.at[slot],
            recv_sem=self.receive.at[slot], device_id=(device,), device_id_type=MESH,
        )

    def partners(self):
        place = self.place
        return [place.sibling, place.along_x, place.along_y] + [place.plane(k) for k in range(1, PLANES)]

    def first(self):
        self.partial[0] = self.value[...]
        self.swap(0, self.place.sibling).start()

    def step(self, at):
        partners = self.partners()
        self.swap(at, partners[at]).wait_recv()
        self.partial[at + 1] = self.partial[at] + self.received[at]
        for slot in (at + 1,) if at < 2 else (3, 4, 5):
            self.swap(slot, partners[slot]).start()

    def finish(self):
        partners = self.partners()
        for slot in (3, 4, 5):
            self.swap(slot, partners[slot]).wait_recv()
        place = self.place
        self.received[6] = self.partial[3]
        total = jnp.zeros_like(self.value)
        for z in range(PLANES):
            behind = (place.z + PLANES - z) % PLANES
            total = total + self.received[(behind + 3) % PLANES + 3]
        self.out[...] = total
        for slot in range(6):
            self.swap(slot, partners[slot]).wait_send()


def reduce_kernel(*refs):
    grads, small = refs[:4], refs[4]
    outs, small_out = refs[5:9], refs[9]
    scratch = refs[10:]
    buffers, (partial, received, send, receive) = scratch[:-4], scratch[-4:]
    place = Place()
    place.meet()
    per = len(FOLD_BUFFERS)
    folds = [
        Fold(place, grads[i], outs[i], *buffers[per * i : per * (i + 1)], send.at[i], receive.at[i]) for i in range(4)
    ]
    share = Share(place, small, small_out, partial, received, send.at[4], receive.at[4])
    steps = [[f.first, f.second, f.third, f.fourth, f.fifth] for f in folds]
    extra = [share.first] + [functools.partial(share.step, at) for at in range(3)] + [share.finish]
    depth = len(steps[0])
    for tick in range(len(folds) + depth - 1):
        for phase in reversed(range(depth)):
            if 0 <= tick - phase < len(folds):
                steps[tick - phase][phase]()
        if tick < len(extra):
            extra[tick]()
    for fold in folds:
        fold.last()


def reduce_grads(grads, small):
    rows = [g.shape[0] // DEVICES for g in grads]
    split = [g.reshape(PLANES, COLUMNS, CORES, n, g.shape[-1]) for g, n in zip(grads, rows)]
    shapes = [(n, g.shape[-1]) for g, n in zip(grads, rows)]
    vmem = pl.BlockSpec(memory_space=pltpu.VMEM)
    return pl.pallas_call(
        reduce_kernel,
        in_specs=[pl.BlockSpec(memory_space=pl.ANY)] * 4 + [vmem],
        out_specs=[vmem] * 5,
        out_shape=[shaped(s, F32) for s in shapes] + [shaped(small.shape, F32)],
        scratch_shapes=[pltpu.VMEM(lead + s, BF16) for s in shapes for lead in FOLD_BUFFERS]
        + [pltpu.VMEM((4,) + small.shape, F32), pltpu.VMEM((7,) + small.shape, F32)]
        + [pltpu.SemaphoreType.DMA((5, Fold.SEMAPHORES))] * 2,
        compiler_params=params(collective_id=1, has_side_effects=True),
    )(*split, small)


def on_device(
    by_kernel,
    hidden, teacher_input, cotangent, lengths, lat_qkv, lat_out, lat_up, lat_down,
    bias_q, bias_v, bias_out, bias_up, bias_down, gain_one, shift_one, gain_two, shift_two, clips,
    teach_qkv, teach_out, teach_up, teach_down,
):
    latent = (lat_qkv, lat_out, lat_up, lat_down)
    teach = (teach_qkv, teach_out, teach_up, teach_down)
    if by_kernel:
        teach, (w_qkv, w_out, w_up, w_down) = gather_weights(teach, latent)
    else:
        gather = functools.partial(lax.all_gather, axis_name="shard", axis=0, tiled=True)
        teach = [gather(w) for w in teach]
        w_qkv, w_out, w_up, w_down = (gather(signed_mean(w)) for w in latent)
    tqk, final = teacher_pass(lengths, teacher_input, *teach)
    qkv, context, logs = student_attend(lengths, clips, hidden, w_qkv, bias_q, bias_v)
    vectors = jnp.concatenate(
        [
            bias_out.reshape(1, D), bias_up.reshape(CHUNKS, D), bias_down.reshape(1, D), gain_one.reshape(1, D),
            shift_one.reshape(1, D), gain_two.reshape(1, D), shift_two.reshape(1, D), jnp.zeros((S_ROWS - 10, D), F32),
        ]
    )
    mixed, act, d_pre, up_in, d_down, cut, d_attn, d_res, d_context, sums = student_middle(
        lengths, clips, hidden, cotangent, final, context, w_out, w_up, w_down, vectors
    )
    g_down, g_up, g_out = weight_grads(act, d_down, up_in, d_pre, cut, d_attn)
    input_grad, g_qkv, q_sums = student_back(lengths, clips, hidden, qkv, tqk, logs, d_context, d_res, w_qkv)
    small = jnp.concatenate([sums, q_sums])
    if by_kernel:
        g_down, g_up, g_qkv, g_out, small = reduce_grads((g_down, g_up, g_qkv, g_out), small)
    else:
        scatter = functools.partial(lax.psum_scatter, axis_name="shard", scatter_dimension=0, tiled=True)
        g_down, g_up, g_qkv, g_out = (scatter(g.astype(F32)) for g in (g_down, g_up, g_qkv, g_out))
        small = lax.psum(small, "shard")
    g_clips = jnp.stack([jnp.sum(small[at]) for at in (S_ROWS + Q_CLIP, S_CLIP_ONE, S_CLIP_TWO, S_CLIP_THREE)])
    return (
        mixed, input_grad, g_qkv, g_out, g_up, g_down,
        small[S_ROWS + Q_QUERY], small[S_ROWS + Q_VALUE], small[S_OUT], small[S_UP : S_UP + CHUNKS].reshape(FF),
        small[S_DOWN], small[S_GAIN_ONE], small[S_SHIFT_ONE], small[S_GAIN_TWO], small[S_SHIFT_TWO], g_clips,
    )


def solution(mesh):
    split, rows, same = P("shard", None), P("shard", None, None), P()
    return jax.shard_map(
        functools.partial(on_device, mesh.shape["shard"] == DEVICES),
        mesh=mesh,
        in_specs=(rows, rows, rows, P("shard")) + (split,) * 4 + (same,) * 10 + (split,) * 4,
        out_specs=(rows, rows) + (split,) * 4 + (same,) * 10,
        check_vma=False,
    )
```

time: 1320 us -> 526 us (0.40)
  matrix products: 620 us -> 0 us
  Pallas kernels: 0 us -> 492 us
  waiting for transfers between devices: 464 us -> 0 us
  local copies, waits for them, and re-layouts: 111 us -> 16.5 us
  blocking collectives: 41.9 us -> 0 us
  other arithmetic: 46.5 us -> 6.33 us
  between operations: 23.2 us -> 1.14 us
    dot_general x43 -> x0, matrix products: 587 us -> none  [the longest x8 199 us: project(): jnp.einsum('rtd,de->rte', left, weight, preferred_element_type=jnp.float32)]
    pallas_call x0 -> x7, Pallas kernels: none -> 492 us  [the longest x1 145 us: gather_weights(): pl.pallas_call(gather_kernel, in_specs=[pl.BlockSpec(memory_space=pl.ANY)...]
    reduce_scatter x4 -> x0, waiting for transfers between devices: 305 us -> none  [the longest x1 142 us: on_device(): lax.psum_scatter(g_w_down, 'shard', scatter_dimension=0, tiled=True)]
    all_gather x8 -> x0, waiting for transfers between devices: 157 us -> none  [the longest x1 47 us: on_device(): lax.all_gather(teach_qkv, 'shard', axis=0, tiled=True)]
    psum x1 -> x0, blocking collectives: 41.9 us -> none  [on_device(): lax.psum((g_b_q, g_b_v, g_b_out, g_b_up, g_b_down, g_gain_one, g_shift_on...]
    dynamic_slice x45 -> x0, local copies, waits for them, and re-layouts: 41.3 us -> none  [on_device(): lax.map(row_attention, (t_queries, t_keys, t_values, live))]
    while x20 -> x0, local copies, waits for them, and re-layouts: 34.2 us -> none  [the longest x4 18.5 us: on_device(): context, log_total = lax.map(row_attention, (queries, keys, values, live))]
    sub x3 -> x0, matrix products: 33 us -> none  [row_attention(): expo = jnp.exp(masked - top)]
  transfers between devices with their start and end apart: 12 -> 0, of which waited for: 7 -> 0; matrix products, arithmetic and copies ran while one was open for 51% -> 0% of each run, Pallas kernels for 0% -> 0%
where the time goes in v1:
time: 526 us; the launch traced here: 516 us
  Pallas kernels  492 us (94%)
  local copies, waits for them, and re-layouts  16.5 us (3%)
  other arithmetic  6.33 us (1%)
    pallas_call x1, Pallas kernels, gather_weights(): pl.pallas_call(gather_kernel, in_specs=[pl.BlockSpec(memory_space=pl.ANY)...  145 us
    pallas_call x1, Pallas kernels, reduce_grads(): pl.pallas_call(reduce_kernel, in_specs=[pl.BlockSpec(memory_space=pl.ANY)...  95.3 us
    pallas_call x1, Pallas kernels, student_back(): pl.pallas_call(student_back_kernel, grid=(rows,), in_specs=[smem_spec(),...  71.8 us
    pallas_call x1, Pallas kernels, student_middle(): pl.pallas_call(student_middle_kernel, grid=(rows, tokens // block), in_sp...  62.9 us
    pallas_call x1, Pallas kernels, teacher_pass(): pl.pallas_call(teacher_kernel, grid=(rows,), in_specs=[smem_spec(), rows_...  57.2 us
    pallas_call x1, Pallas kernels, student_attend(): pl.pallas_call(student_attend_kernel, grid=(rows,), in_specs=[smem_spec()...  35.4 us
    pallas_call x1, Pallas kernels, weight_grads(): pl.pallas_call(weight_grads_kernel, grid=(CHUNKS,), in_specs=[chunk, same...  24.8 us

profile of v1, /device:TPU:0, one launch (start us, length us, event | category | flops | bytes accessed | tf_op | source)
XLA Modules:
  0.0 516.2 jit_solution(2212314760596030499)
XLA Ops:
  0.6 1.3 reshape.121.bias_q
  1.9 1.3 reshape.122.bias_v
  3.2 0.7 reshape.126
  3.9 0.7 reshape.128
  4.6 0.7 reshape.129
  5.2 0.7 reshape.130
  5.9 0.7 reshape.131
  7.3 0.7 reshape.127
  8.0 1.3 concatenate.6.vectors
  9.3 144.7 %shard_map.333 = (bf16[4,8,24,2304]{3,2,1,0:T(8,128)(2,1)}, bf16[4,8,24,768]{3,2,1,0:T(8,128)(2,1)}, bf16[4,8,24,3072]{3,2,1,0:T(8,128)(2,1)}, bf16[4,8,96,768]{...) custom-call(bf16[24,2304]{1,0:T(8,128)(2,1)} %refs_0_.1, ...), custom_call_target="tpu_custom_call" | custom-call | tf_op jit(solution)/shard_map/pallas_call | solution.py:522
  154.0 57.2 %shard_map.334 = (bf16[3,512,1536]{2,1,0:T(8,128)(2,1)}, f32[3,512,768]{2,1,0:T(8,128)}) custom-call(s32[3]{0:T(128)} %lengths.7, bf16[3,512,768]{2,1,0:T(8,128)(2,1)} %x_ref.4, bf16[768,2304]{1,0:T(8,128)(2,1)} %bitcast.33, bf16[768,768]{1,0:T(8,128)(2,1)} %bitcast.40, bf16[768,3072]{1,0:T(8,128)(2,1)} %bitcast.28, bf16[3072,768]{1,0:T(8,128)(2,1)} %bitcast.29), custom_call_target="tpu_custom_call" | custom-call | tf_op jit(solution)/shard_map/pallas_call | solution.py:310
  211.2 35.4 %shard_map.335 = (bf16[3,512,2304]{2,1,0:T(8,128)(2,1)}, f32[3,512,768]{2,1,0:T(8,128)}, f32[3,6,2,512]{3,2,1,0:T(2,128)}) custom-call(s32[3]{0:T(128)} %lengths.7, f32[4]{0:T(128)} %clips.5, bf16[3,512,768]{2,1,0:T(8,128)(2,1)} %x_ref.7, bf16[768,2304]{1,0:T(8,128)(2,1)} %bitcast.22, f32[1,768]{1,0:T(1,128)} %reshape.121.bias_q, f32[1,768]{1,0:T(1,128)} %reshape.122.bias_v), custom_call_target="tpu_custom_call" | custom-call | tf_op jit(solution)/shard_map/pallas_call | solution.py:324
  246.6 62.9 %shard_map.336 = (bf16[3,512,768]{2,1,0:T(8,128)(2,1)}, bf16[3,512,3072]{2,1,0:T(8,128)(2,1)}, bf16[3,512,3072]{2,1,0:T(8,128)(2,1)}, bf16[3,512,768]{2,1,0:T(8,...) custom-call(s32[3]{0:T(128)} %lengths.7, f32[4]{0:T(128)} %clips.5, ...), custom_call_target="tpu_custom_call" | custom-call | tf_op jit(solution)/shard_map/pallas_call | solution.py:351
  309.6 71.8 %shard_map.337 = (bf16[3,512,768]{2,1,0:T(8,128)(2,1)}, bf16[768,2304]{1,0:T(8,128)(2,1)}, f32[8,768]{1,0:T(8,128)}) custom-call(s32[3]{0:T(128)} %lengths.7, f32[4]{0:T(128)} %clips.5, bf16[3,512,768]{2,1,0:T(8,128)(2,1)} %x_ref.7, bf16[3,512,2304]{2,1,0:T(8,128)(2,1)} %get-tuple-element.61.qkv_ref, bf16[3,512,1536]{2,1,0:T(8,128)(2,1)} %get-tuple-element.62.tqk_ref, ...), custom_call_target="tpu_custom_call" | custom-call | tf_op jit(solution)/shard_map/pallas_call | solution.py:388
  381.4 1.4 pad_maximum_fusion.refs_4_
  382.8 24.8 %shard_map.338 = (bf16[3072,768]{1,0:T(8,128)(2,1)}, bf16[768,3072]{1,0:T(8,128)(2,1)}, bf16[768,768]{1,0:T(8,128)(2,1)}) custom-call(bf16[1536,3072]{1,0:T(8,128)(2,1)} %bitcast.24, bf16[1536,768]{1,0:T(8,128)(2,1)} %bitcast.35, bf16[1536,768]{1,0:T(8,128)(2,1)} %bitcast.34, bf16[1536,3072]{1,0:T(8,128)(2,1)} %bitcast.25, bf16[1536,768]{1,0:T(8,128)(2,1)} %bitcast.36, ...), custom_call_target="tpu_custom_call" | custom-call | tf_op jit(solution)/shard_map/pallas_call | solution.py:372
  407.6 95.3 %shard_map.339 = (f32[96,768]{1,0:T(8,128)}, f32[24,3072]{1,0:T(8,128)}, f32[24,2304]{1,0:T(8,128)}, f32[24,768]{1,0:T(8,128)}, f32[24,768]{1,0:T(8,128)}) custom-call(bf16[4,4,2,96,768]{4,3,2,1,0:T(8,128)(2,1)} %bitcast.26, bf16[4,4,2,24,3072]{4,3,2,1,0:T(8,128)(2,1)} %bitcast.27, bf16[4,4,2,24,2304]{4,3,2,1,0:T(8,128)(2,1)} %bitcast.32, ...), custom_call_target="tpu_custom_call" | custom-call | tf_op jit(solution)/shard_map/pallas_call | solution.py:704
  502.9 0.7 slice.42
  503.6 1.8 slice_reduce_fusion.3
  506.0 3.2 pad_maximum_fusion.1
  509.2 1.6 copy.42
  510.8 1.5 copy.43
  512.4 1.7 copy.44
  514.1 1.7 copy.45
  (5 shorter events, 1.3 us)
Async XLA Ops:
  309.6 71.8 %copy-start = (f32[16,768]{1,0:T(8,128)S(1)}, f32[16,768]{1,0:T(8,128)}, u32[]{:S(2)}) copy-start(f32[16,768]{1,0:T(8,128)} %get-tuple-element.77) | copy-start | bytes 147460
